TPU v7x, 32 devices: a whole 2x2x4 slice. The times are simulated.
32 devices in a mesh: row: 4 (over y, x), col: 8 (over z, core).
Axes of the slice: x: 2, y: 2, z: 4, core: 2. Of those that a mesh axis runs over, the one named last changes fastest.
Arguments:
- trail: float32 [2, 4, 512, 2, 8, 512], P(None, 'row', None, None, 'col'), may hold values from -6 to 6
- panel: float32 [2, 4, 512, 512], P(None, 'row', None, 'col'), may hold values from -6 to 6
- row_basis: float32 [2, 4, 64, 512], P(None, 'row', None, 'col'), may hold values from -0.75 to 0.75
- row_coeff: float32 [2, 4, 64, 512], P(None, 'row', None, 'col'), may hold values from -0.25 to 0.25
- col_basis: float32 [2, 8, 64, 512], P(None, 'col', None, 'row'), may hold values from -0.75 to 0.75
- col_scaled: float32 [2, 8, 64, 512], P(None, 'col', None, 'row'), may hold values from -0.25 to 0.25
- pivot_basis: float32 [64, 512], P(None, 'col'), may hold values from -0.75 to 0.75
- pivot_scaled: float32 [64, 512], replicated, may hold values from -0.25 to 0.25
- sketch: float32 [64, 512], replicated, may hold values from -6 to 6
- perm: int32 [512], replicated, may hold values from 0 to 511, each once
- pair_kind: int32 [256], replicated, may hold values from 0 to 1
- pivot_values: float32 [3, 256], replicated, may hold values from -3 to 3, as said below
Outputs:
- trail_out: float32 [2, 4, 512, 2, 8, 512], P(None, 'row', None, None, 'col')
- basis_out: float32 [2, 4, 64, 512], P(None, 'row')
- coeff_out: float32 [2, 4, 64, 512], P(None, 'row')
Inputs may be any that keep to these rules, and one draw needn't show every extreme that they name: `pivot_values`: rows 0 and 1 have magnitudes between 0.5 and 0.7; row 2 has magnitude 1.2 or more.
All inputs are finite; a program needn't handle non-finite values.
Results may differ from a plain program's by a relative error of at most 0.00013.
Values sent between devices are 32-bit elements; how exact they have to be, the bound alone decides.
No kernel may reach another device: no remote copies, remote signals or barrier semaphores. Data moves between devices by JAX's collectives and lax.ppermute only.
A program may use at most 64 MiB of HBM per device.

v0:
```python
import jax
import jax.numpy as jnp
from jax import lax
from jax.sharding import PartitionSpec as P


def pair_apply(rows, pair_kind, pivot_values):
    shaped = rows.reshape(rows.shape[:-1] + (rows.shape[-1] // 2, 2))
    first_in = shaped[..., 0]
    second_in = shaped[..., 1]
    diag_one = pivot_values[0]
    diag_two = pivot_values[1]
    offdiag = pivot_values[2]
    determinant = diag_one * diag_two - offdiag * offdiag
    twin = pair_kind == 1
    first = jnp.where(
        twin, (first_in * diag_two - second_in * offdiag) / determinant, first_in / diag_one
    )
    second = jnp.where(
        twin, (second_in * diag_one - first_in * offdiag) / determinant, second_in / diag_two
    )
    return jnp.stack([first, second], axis=-1).reshape(rows.shape)


def tri_solve(lower, rhs):
    return jax.vmap(lambda low, right: jax.scipy.linalg.solve_triangular(low, right, lower=True))(
        lower, rhs
    )


def body(
    trail,
    panel,
    row_basis,
    row_coeff,
    col_basis,
    col_scaled,
    pivot_basis,
    pivot_scaled,
    sketch,
    perm,
    pair_kind,
    pivot_values,
):
    highest = lax.Precision.HIGHEST
    width = sketch.shape[1]
    block = panel.shape[3]
    xrows, yrows = (
        lax.all_gather(row_basis, "col", axis=3, tiled=True),
        lax.all_gather(row_coeff, "col", axis=3, tiled=True),
    )
    zcols, gcols = (
        lax.all_gather(col_basis, "row", axis=3, tiled=True),
        lax.all_gather(col_scaled, "row", axis=3, tiled=True),
    )
    xrows = xrows[:, 0]
    yrows = yrows[:, 0]
    zcols = zcols[:, 0]
    gcols = gcols[:, 0]
    core = jnp.einsum("arp,bsp->arbs", yrows, gcols, precision=highest)
    left = jnp.einsum("arp,arbs->apbs", xrows, core, precision=highest)
    change = jnp.einsum("apbs,bsq->apbq", left, zcols, precision=highest)
    trail_out = trail - change[:, None, :, :, None, :]
    pcore = jnp.einsum("arp,sp->ars", yrows, pivot_scaled, precision=highest)
    pleft = jnp.einsum("arp,ars->aps", xrows, pcore, precision=highest)
    updated = panel[:, 0] - jnp.einsum("aps,sq->apq", pleft, pivot_basis, precision=highest)
    scaled_t = pair_apply(sketch, pair_kind, pivot_values)
    column_ids = lax.axis_index("col") * block + jnp.arange(block, dtype=jnp.int32)
    selector = (perm[:, None] == column_ids[None, :]).astype(jnp.float32)
    local_sketch = jnp.dot(scaled_t, selector, precision=highest)
    partial_range = jnp.einsum("apq,rq->arp", updated, local_sketch, precision=highest)
    range_t = lax.psum(partial_range, "col")
    gram = jnp.einsum("arp,asp->ars", range_t, range_t, precision=highest) / width
    basis = tri_solve(jnp.linalg.cholesky(gram), range_t)
    projected_part = jnp.einsum("arp,apq->arq", basis, updated, precision=highest)
    projected = lax.all_gather(projected_part, "col", axis=2, tiled=True)
    permuted = jnp.take(projected, perm, axis=2)
    coeff = pair_apply(permuted, pair_kind, pivot_values) / jnp.sqrt(jnp.float32(width))
    return (trail_out, basis[:, None], coeff[:, None])


def solution(mesh):
    return jax.shard_map(
        body,
        mesh=mesh,
        in_specs=(
            P(None, "row", None, None, "col", None),
            P(None, "row", None, "col"),
            P(None, "row", None, "col"),
            P(None, "row", None, "col"),
            P(None, "col", None, "row"),
            P(None, "col", None, "row"),
            P(None, "col"),
            P(),
            P(),
            P(),
            P(),
            P(),
        ),
        out_specs=(
            P(None, "row", None, None, "col", None),
            P(None, "row", None, None),
            P(None, "row", None, None),
        ),
        check_vma=False,
    )
```

profile of v0, /device:TPU:0, one launch (start us, length us, event | category | flops | bytes accessed | tf_op | source)
XLA Modules:
  0.0 159.1 jit_solution(12313392400558865005)
XLA Ops:
  7.3 0.8 broadcast_compare_fusion
  8.1 0.8 fusion.16
  8.9 0.9 copy.54
  9.8 0.9 copy.51
  10.8 1.0 copy.59
  11.8 16.5 %all_gather.15 = f32[2,1,64,512]{2,0,1,3:T(2,128)S(1)} all-gather(f32[2,1,64,64]{2,0,1,3:T(2,128)S(1)} %copy.51), channel_id=1, replica_groups=mesh['row'=4,'col'=8] {'col'}, dimensions={3}, use_global_device_ids=true | all-gather | bytes 294912 | tf_op jit(solution)/shard_map/all_gather | solution.py:50
  28.5 14.8 %all_gather.17 = f32[2,1,64,512]{2,0,1,3:T(2,128)S(1)} all-gather(f32[2,1,64,64]{2,0,1,3:T(2,128)S(1)} %copy.54), channel_id=1, replica_groups=mesh['row'=4,'col'=8] {'col'}, dimensions={3}, use_global_device_ids=true | all-gather | bytes 294912 | tf_op jit(solution)/shard_map/all_gather | solution.py:49
  43.5 2.2 %broadcast_select_fusion.4 = (f32[64,256,1]{0,2,1:T(1,128)S(1)}, f32[64,256,1]{0,2,1:T(1,128)S(1)}) fusion(pred[256]{0:T(512)(128)(4,1)S(1)} %broadcast_compare_fusion, f32[64,256,2]{0,2,1:T(2,128)S(1)} %bitcast.82, f32[256]{0:T(256)S(1)} %bitcast.90, f32[256]{0:T(256)S(1)} %bitcast.96, f32[256]{0:T(256)S(1)} %bitcast.93, f32[256]{0:T(256)S(1)} %bitcast.87), kind=kLoop, calls=%fused_computation.21 | loop fusion | flops 196608 | bytes 266496 | tf_op jit(solution)/shard_map/jit(_where)/select_n | solution.py:16
  47.7 1.1 convolution_bitcast_fusion.1
  48.9 10.3 %all_gather.18 = f32[2,1,64,512]{3,2,0,1:T(8,128)S(1)} all-gather(f32[2,1,64,128]{3,2,0,1:T(8,128)S(1)} %bitcast.85), channel_id=1, replica_groups=mesh['row'=4,'col'=8] {'row'}, dimensions={3}, use_global_device_ids=true | all-gather | bytes 327680 | tf_op jit(solution)/shard_map/all_gather | solution.py:53
  59.2 10.2 %all_gather.16 = f32[2,1,64,512]{3,2,0,1:T(8,128)S(1)} all-gather(f32[2,1,64,128]{3,2,0,1:T(8,128)S(1)} %bitcast.86), channel_id=1, replica_groups=mesh['row'=4,'col'=8] {'row'}, dimensions={3}, use_global_device_ids=true | all-gather | bytes 327680 | tf_op jit(solution)/shard_map/all_gather | solution.py:54
  69.9 0.6 convolution_bitcast_fusion
  70.5 7.2 %bitcast_subtract_fusion = f32[2,1,512,2,1,512]{5,2,0,3,4,1:T(8,128)} fusion(f32[2,1,512,2,1,512]{5,4,3,2,1,0:T(1,128)} %param.12, f32[2,512,2,64]{1,3,0,2:T(8,128)S(1)} %convolution_bitcast_fusion, f32[2,1,64,512]{3,2,0,1:T(8,128)S(1)} %all_gather.18), kind=kOutput, calls=%fused_computation.1 | convolution fusion | flops 806354944 | bytes 9175040 | tf_op jit(solution)/shard_map/apbs,bsq->apbq/dot_general | solution.py:62
  77.9 8.5 %copy.66 = f32[2,1,512,2,1,512]{5,4,3,2,1,0:T(1,128)} copy(f32[2,1,512,2,1,512]{5,2,0,3,4,1:T(8,128)} %bitcast_subtract_fusion) | data formatting | bytes 8388608
  86.4 19.4 %all-reduce.2.cloned.1.call-done = f32[2,64,512]{2,1,0:T(8,128)} async-done(((f32[2,64,512]{2,1,0:T(8,128)}), f32[2,64,512]{2,1,0:T(8,128)}) %all-reduce.2.cloned.1.call-update) | async-done | bytes 262160 | tf_op jit(solution)/shard_map/psum | solution.py:72
  105.8 1.4 fusion.17
  107.3 11.7 %custom-call.8 = f32[2,64,64]{2,1,0:T(8,128)S(1)} custom-call(f32[2,64,64]{2,1,0:T(8,128)S(1)} %fusion.14), custom_call_target="Cholesky" | custom-call | tf_op jit(solution)/shard_map/jit(cholesky)/cholesky | solution.py:74
  119.3 9.8 %custom-call.9 = f32[2,1,64,64]{2,3,1,0:T(8,128)S(1)} custom-call(f32[2,1,64,64]{3,2,1,0:T(8,128)S(1)} %select_bitcast_fusion), custom_call_target="InvertDiagBlocksLowerTriangular" | custom-call | tf_op jit(solution)/shard_map/vmap(jit(_solve_triangular))/triangular_solve | solution.py:26
  129.1 1.4 fusion.12
  131.0 15.1 %all_gather.19 = f32[2,64,512]{1,0,2:T(2,128)S(1)} all-gather(f32[2,64,64]{1,0,2:T(2,128)S(1)} %copy.64), channel_id=1, replica_groups=mesh['row'=4,'col'=8] {'col'}, dimensions={2}, use_global_device_ids=true | all-gather | bytes 294912 | tf_op jit(solution)/shard_map/all_gather | solution.py:76
  146.1 2.1 %gather_fusion = f32[512,2,64]{2,1,0:T(2,128)S(1)} fusion(f32[2,64,512]{1,0,2:T(2,128)S(1)} %all_gather.19, s32[1024]{0:T(1024)S(1)} %pad_clamp_fusion), kind=kCustom, calls=%fused_computation | custom fusion | bytes 526336 | tf_op jit(solution)/shard_map/jit(_take)/gather | solution.py:77
  148.6 2.2 %broadcast_select_fusion.1 = (f32[2,64,256,1]{1,3,2,0:T(1,128)S(1)}, f32[2,64,256,1]{1,3,2,0:T(1,128)S(1)}) fusion(pred[256]{0:T(512)(128)(4,1)S(1)} %broadcast_compare_fusion, f32[2,64,256,2]{1,3,2,0:T(2,128)S(1)} %broadcast_select_fusion.2, f32[256]{0:T(256)S(1)} %bitcast.92, f32[256]{0:T(256)S(1)} %multiply_subtract_fusion, f32[256]{0:T(256)S(1)} %bitcast.95, ...), kind=kLoop, calls=%fused_computation.9 | loop fusion | flops 393216 | bytes 528640 | tf_op jit(solution)/shard_map/jit(_where)/select_n | solution.py:16
  150.8 0.6 maximum_multiply_fusion
  151.4 0.9 copy.68
  (41 shorter events, 4.4 us)
Async XLA Ops:
  7.2 38.8 %copy-start = (f32[64,512]{1,0:T(8,128)S(1)}, f32[64,512]{1,0:T(8,128)}, u32[]{:S(2)}) copy-start(f32[64,512]{1,0:T(8,128)} %param.19) | copy-start | bytes 393220
  7.2 39.7 %copy-start.6 = (s32[512]{0:T(512)S(1)}, s32[512]{0:T(512)}, u32[]{:S(2)}) copy-start(s32[512]{0:T(512)} %param.21) | copy-start | bytes 6148
  7.2 40.1 %copy-start.5 = (f32[64,64]{1,0:T(8,128)S(1)}, f32[64,64]{1,0:T(8,128)}, u32[]{:S(2)}) copy-start(f32[64,64]{1,0:T(8,128)} %param.18) | copy-start | bytes 49156
  7.2 40.1 %copy-start.2 = (f32[2,1,512,64]{2,3,1,0:T(8,128)S(1)}, f32[2,1,512,64]{2,3,1,0:T(8,128)}, u32[]{:S(2)}) copy-start(f32[2,1,512,64]{2,3,1,0:T(8,128)} %param.13) | copy-start | bytes 786436
  7.2 41.7 %copy-start.3 = (f32[2,1,64,128]{3,2,1,0:T(8,128)S(1)}, f32[2,1,64,128]{3,2,1,0:T(8,128)}, u32[]{:S(2)}) copy-start(f32[2,1,64,128]{3,2,1,0:T(8,128)} %param.16) | copy-start | bytes 196612
  7.2 52.0 %copy-start.4 = (f32[2,1,64,128]{3,2,1,0:T(8,128)S(1)}, f32[2,1,64,128]{3,2,1,0:T(8,128)}, u32[]{:S(2)}) copy-start(f32[2,1,64,128]{3,2,1,0:T(8,128)} %param.17) | copy-start | bytes 196612
  7.2 98.6 %all-reduce.2.cloned.1.call-start = ((), (), s32[]{:S(2)}) async-start(), calls=%async_computation | async-start | bytes 524288 | tf_op jit(solution)/shard_map/psum | solution.py:72
  130.5 21.8 %copy-start.1 = (f32[2,64,512]{2,1,0:T(8,128)}, f32[2,64,512]{2,1,0:T(8,128)S(1)}, u32[]{:S(2)}) copy-start(f32[2,64,512]{2,1,0:T(8,128)S(1)} %fusion.12) | copy-start | bytes 786436
Sparse Core Ops, SparseCore 0:
  49.0 56.7 all-reduce.1
where the time goes:
time: 160 us; the launch traced here: 159 us
  blocking collectives  66.8 us (42%)
  other arithmetic  29.1 us (18%)
  waiting for transfers between devices  19.4 us (12%)
  local copies, waits for them, and re-layouts  15.2 us (10%)
  between operations  14.4 us (9%)
  matrix products  14.3 us (9%)
    psum x1, waiting for transfers between devices, body(): range_t = lax.psum(partial_range, 'col')  19.4 us
    all_gather x1, blocking collectives, body(): lax.all_gather(row_coeff, 'col', axis=3, tiled=True)  16.5 us
    all_gather x1, blocking collectives, body(): projected = lax.all_gather(projected_part, 'col', axis=2, tiled=True)  15.1 us
    all_gather x1, blocking collectives, body(): lax.all_gather(row_basis, 'col', axis=3, tiled=True)  14.8 us
    unnamed x19, local copies, waits for them, and re-layouts  12.3 us
    another operation x4, other arithmetic, body(): basis = tri_solve(jnp.linalg.cholesky(gram), range_t)  11.9 us
    all_gather x1, blocking collectives, body(): lax.all_gather(col_basis, 'row', axis=3, tiled=True)  10.3 us
    all_gather x1, blocking collectives, body(): lax.all_gather(col_scaled, 'row', axis=3, tiled=True)  10.2 us
  transfers between devices with their start and end apart: 1, of which 1 were waited for; matrix products, arithmetic and copies ran while one was open for 11% of the time, Pallas kernels for 0%

commit v1 on v0

--- a/solution.py
+++ b/solution.py
@@ -73,7 +73,12 @@
     gram = jnp.einsum("arp,asp->ars", range_t, range_t, precision=highest) / width
     basis = tri_solve(jnp.linalg.cholesky(gram), range_t)
     projected_part = jnp.einsum("arp,apq->arq", basis, updated, precision=highest)
-    projected = lax.all_gather(projected_part, "col", axis=2, tiled=True)
+    ring = [projected_part]
+    for hop in range(7):
+        ring.append(lax.ppermute(ring[-1], "col", [(dev, (dev + 1) % 8) for dev in range(8)]))
+    projected = jnp.roll(
+        jnp.concatenate(ring[::-1], axis=2), (lax.axis_index("col") + 1) * ring[0].shape[2], axis=2
+    )
     permuted = jnp.take(projected, perm, axis=2)
     coeff = pair_apply(permuted, pair_kind, pivot_values) / jnp.sqrt(jnp.float32(width))
     return (trail_out, basis[:, None], coeff[:, None])

time: 160 us -> 193 us (1.21)
  waiting for transfers between devices: 19.4 us -> 67.3 us
  blocking collectives: 66.8 us -> 51.6 us
    psum x1, waiting for transfers between devices: 19.4 us -> 46 us  [body(): range_t = lax.psum(partial_range, 'col')]
    ppermute x0 -> x7, waiting for transfers between devices: none -> 21.3 us  [body(): lax.ppermute(ring[-1], 'col', [(dev, (dev + 1) % 8) for dev in range(8)])]
    all_gather x1 -> x0, blocking collectives: 15.1 us -> none  [body(): projected = lax.all_gather(projected_part, 'col', axis=2, tiled=True)]
  transfers between devices with their start and end apart: 1 -> 8, of which waited for: 1 -> 5; matrix products, arithmetic and copies ran while one was open for 11% -> 9% of each run, Pallas kernels for 0% -> 0%
where the time goes in v1:
time: 193 us
  waiting for transfers between devices  67.3 us (35%)
  blocking collectives  51.6 us (27%)
  other arithmetic  29.1 us (15%)
  local copies, waits for them, and re-layouts  15.7 us (8%)
  between operations  14.4 us (7%)
  matrix products  14.3 us (7%)
    psum x1, waiting for transfers between devices, body(): range_t = lax.psum(partial_range, 'col')  46 us
    ppermute x7, waiting for transfers between devices, body(): lax.ppermute(ring[-1], 'col', [(dev, (dev + 1) % 8) for dev in range(8)])  21.3 us
    all_gather x1, blocking collectives, body(): lax.all_gather(row_coeff, 'col', axis=3, tiled=True)  16.5 us
    all_gather x1, blocking collectives, body(): lax.all_gather(row_basis, 'col', axis=3, tiled=True)  14.8 us
    unnamed x19, local copies, waits for them, and re-layouts  12.3 us
    another operation x4, other arithmetic, body(): basis = tri_solve(jnp.linalg.cholesky(gram), range_t)  11.9 us
    all_gather x1, blocking collectives, body(): lax.all_gather(col_scaled, 'row', axis=3, tiled=True)  10.3 us
    all_gather x1, blocking collectives, body(): lax.all_gather(col_basis, 'row', axis=3, tiled=True)  9.99 us
  transfers between devices with their start and end apart: 8, of which 5 were waited for; matrix products, arithmetic and copies ran while one was open for 9% of the time, Pallas kernels for 0%

profile of v1, /device:TPU:0, one launch (start us, length us, event | category | flops | bytes accessed | tf_op | source)
XLA Modules:
  0.0 192.6 jit_solution(4957277382161737081)
XLA Ops:
  8.1 0.8 fusion.16
  8.9 0.9 copy.54
  9.8 0.9 copy.51
  10.7 1.0 copy.59
  11.8 16.5 %all_gather.12 = f32[2,1,64,512]{2,0,1,3:T(2,128)S(1)} all-gather(f32[2,1,64,64]{2,0,1,3:T(2,128)S(1)} %copy.51), channel_id=1, replica_groups=mesh['row'=4,'col'=8] {'col'}, dimensions={3}, use_global_device_ids=true | all-gather | bytes 294912 | tf_op jit(solution)/shard_map/all_gather | solution.py:50
  28.5 14.8 %all_gather.14 = f32[2,1,64,512]{2,0,1,3:T(2,128)S(1)} all-gather(f32[2,1,64,64]{2,0,1,3:T(2,128)S(1)} %copy.54), channel_id=1, replica_groups=mesh['row'=4,'col'=8] {'col'}, dimensions={3}, use_global_device_ids=true | all-gather | bytes 294912 | tf_op jit(solution)/shard_map/all_gather | solution.py:49
  43.5 2.2 %broadcast_select_fusion.4 = (f32[64,256,1]{0,2,1:T(1,128)S(1)}, f32[64,256,1]{0,2,1:T(1,128)S(1)}) fusion(pred[256]{0:T(512)(128)(4,1)S(1)} %broadcast_compare_fusion, f32[64,256,2]{0,2,1:T(2,128)S(1)} %bitcast.82, f32[256]{0:T(256)S(1)} %bitcast.90, f32[256]{0:T(256)S(1)} %bitcast.96, f32[256]{0:T(256)S(1)} %bitcast.93, f32[256]{0:T(256)S(1)} %bitcast.87), kind=kLoop, calls=%fused_computation.21 | loop fusion | flops 196608 | bytes 266496 | tf_op jit(solution)/shard_map/jit(_where)/select_n | solution.py:16
  47.7 1.1 convolution_bitcast_fusion.1
  48.8 10.3 %all_gather.13 = f32[2,1,64,512]{3,2,0,1:T(8,128)S(1)} all-gather(f32[2,1,64,128]{3,2,0,1:T(8,128)S(1)} %bitcast.85), channel_id=1, replica_groups=mesh['row'=4,'col'=8] {'row'}, dimensions={3}, use_global_device_ids=true | all-gather | bytes 327680 | tf_op jit(solution)/shard_map/all_gather | solution.py:54
  59.7 46.0 %all-reduce.2.cloned.1.call-done = f32[2,64,512]{2,1,0:T(8,128)} async-done(((f32[2,64,512]{2,1,0:T(8,128)}), f32[2,64,512]{2,1,0:T(8,128)}) %all-reduce.2.cloned.1.call-update) | async-done | bytes 262160 | tf_op jit(solution)/shard_map/psum | solution.py:72
  105.8 1.4 fusion.17
  107.3 11.7 %custom-call.8 = f32[2,64,64]{2,1,0:T(8,128)S(1)} custom-call(f32[2,64,64]{2,1,0:T(8,128)S(1)} %fusion.14), custom_call_target="Cholesky" | custom-call | tf_op jit(solution)/shard_map/jit(cholesky)/cholesky | solution.py:74
  119.2 9.8 %custom-call.9 = f32[2,1,64,64]{2,3,1,0:T(8,128)S(1)} custom-call(f32[2,1,64,64]{3,2,1,0:T(8,128)S(1)} %select_bitcast_fusion), custom_call_target="InvertDiagBlocksLowerTriangular" | custom-call | tf_op jit(solution)/shard_map/vmap(jit(_solve_triangular))/triangular_solve | solution.py:26
  129.1 1.4 fusion.12
  131.5 4.9 %collective-permute-done = f32[2,64,64]{2,1,0:T(8,128)S(1)} collective-permute-done((f32[2,64,64]{2,1,0:T(8,128)S(1)}, f32[2,64,64]{2,1,0:T(8,128)S(1)}, u32[]{:S(2)}, u32[]{:S(2)}) %collective-permute-start) | collective-permute-done | bytes 32800 | tf_op jit(solution)/shard_map/ppermute | solution.py:78
  136.4 10.0 %all_gather.15 = f32[2,1,64,512]{3,2,0,1:T(8,128)S(1)} all-gather(f32[2,1,64,128]{3,2,0,1:T(8,128)S(1)} %bitcast.86), channel_id=1, replica_groups=mesh['row'=4,'col'=8] {'row'}, dimensions={3}, use_global_device_ids=true | all-gather | bytes 327680 | tf_op jit(solution)/shard_map/all_gather | solution.py:53
  146.4 7.2 %bitcast_subtract_fusion = f32[2,1,512,2,1,512]{5,2,0,3,4,1:T(8,128)} fusion(f32[2,1,512,2,1,512]{5,4,3,2,1,0:T(1,128)} %param.12, f32[2,512,2,64]{1,3,0,2:T(8,128)S(1)} %convolution_bitcast_fusion, f32[2,1,64,512]{3,2,0,1:T(8,128)S(1)} %all_gather.15), kind=kOutput, calls=%fused_computation.1 | convolution fusion | flops 806354944 | bytes 9175040 | tf_op jit(solution)/shard_map/apbs,bsq->apbq/dot_general | solution.py:62
  153.7 5.4 %collective-permute-done.3 = f32[2,64,64]{2,1,0:T(8,128)S(1)} collective-permute-done((f32[2,64,64]{2,1,0:T(8,128)S(1)}, f32[2,64,64]{2,1,0:T(8,128)S(1)}, u32[]{:S(2)}, u32[]{:S(2)}) %collective-permute-start.3) | collective-permute-done | bytes 32800 | tf_op jit(solution)/shard_map/ppermute | solution.py:78
  159.1 5.5 %collective-permute-done.4 = f32[2,64,64]{2,1,0:T(8,128)S(1)} collective-permute-done((f32[2,64,64]{2,1,0:T(8,128)S(1)}, f32[2,64,64]{2,1,0:T(8,128)S(1)}, u32[]{:S(2)}, u32[]{:S(2)}) %collective-permute-start.4) | collective-permute-done | bytes 32800 | tf_op jit(solution)/shard_map/ppermute | solution.py:78
  164.6 5.5 %collective-permute-done.5 = f32[2,64,64]{2,1,0:T(8,128)S(1)} collective-permute-done((f32[2,64,64]{2,1,0:T(8,128)S(1)}, f32[2,64,64]{2,1,0:T(8,128)S(1)}, u32[]{:S(2)}, u32[]{:S(2)}) %collective-permute-start.5) | collective-permute-done | bytes 32800 | tf_op jit(solution)/shard_map/ppermute | solution.py:78
  170.3 8.5 %copy.66 = f32[2,1,512,2,1,512]{5,4,3,2,1,0:T(1,128)} copy(f32[2,1,512,2,1,512]{5,2,0,3,4,1:T(8,128)} %bitcast_subtract_fusion) | data formatting | bytes 8388608
  179.5 2.1 %gather_fusion = f32[512,2,64]{2,1,0:T(2,128)S(1)} fusion(f32[2,64,512]{1,0,2:T(2,128)S(1)} %copy.64, s32[1024]{0:T(1024)S(1)} %pad_clamp_fusion), kind=kCustom, calls=%fused_computation | custom fusion | bytes 526336 | tf_op jit(solution)/shard_map/jit(_take)/gather | solution.py:82
  182.0 2.2 %broadcast_select_fusion.1 = (f32[2,64,256,1]{1,3,2,0:T(1,128)S(1)}, f32[2,64,256,1]{1,3,2,0:T(1,128)S(1)}) fusion(pred[256]{0:T(512)(128)(4,1)S(1)} %broadcast_compare_fusion, f32[2,64,256,2]{1,3,2,0:T(2,128)S(1)} %broadcast_select_fusion.2, f32[256]{0:T(256)S(1)} %bitcast.92, f32[256]{0:T(256)S(1)} %multiply_subtract_fusion, f32[256]{0:T(256)S(1)} %bitcast.95, ...), kind=kLoop, calls=%fused_computation.9 | loop fusion | flops 393216 | bytes 528640 | tf_op jit(solution)/shard_map/jit(_where)/select_n | solution.py:16
  184.8 0.9 copy.68
  (56 shorter events, 7.2 us)
Async XLA Ops:
  7.2 38.8 %copy-start = (f32[64,512]{1,0:T(8,128)S(1)}, f32[64,512]{1,0:T(8,128)}, u32[]{:S(2)}) copy-start(f32[64,512]{1,0:T(8,128)} %param.19) | copy-start | bytes 393220
  7.2 39.6 %copy-start.6 = (s32[512]{0:T(512)S(1)}, s32[512]{0:T(512)}, u32[]{:S(2)}) copy-start(s32[512]{0:T(512)} %param.21) | copy-start | bytes 6148
  7.2 40.1 %copy-start.5 = (f32[64,64]{1,0:T(8,128)S(1)}, f32[64,64]{1,0:T(8,128)}, u32[]{:S(2)}) copy-start(f32[64,64]{1,0:T(8,128)} %param.18) | copy-start | bytes 49156
  7.2 40.1 %copy-start.2 = (f32[2,1,512,64]{2,3,1,0:T(8,128)S(1)}, f32[2,1,512,64]{2,3,1,0:T(8,128)}, u32[]{:S(2)}) copy-start(f32[2,1,512,64]{2,3,1,0:T(8,128)} %param.13) | copy-start | bytes 786436
  7.2 41.6 %copy-start.3 = (f32[2,1,64,128]{3,2,1,0:T(8,128)S(1)}, f32[2,1,64,128]{3,2,1,0:T(8,128)}, u32[]{:S(2)}) copy-start(f32[2,1,64,128]{3,2,1,0:T(8,128)} %param.17) | copy-start | bytes 196612
  7.2 98.5 %all-reduce.2.cloned.1.call-start = ((), (), s32[]{:S(2)}) async-start(), calls=%async_computation | async-start | bytes 524288 | tf_op jit(solution)/shard_map/psum | solution.py:72
  43.4 93.0 %copy-start.4 = (f32[2,1,64,128]{3,2,1,0:T(8,128)S(1)}, f32[2,1,64,128]{3,2,1,0:T(8,128)}, u32[]{:S(2)}) copy-start(f32[2,1,64,128]{3,2,1,0:T(8,128)} %param.16) | copy-start | bytes 196612
  130.5 23.1 %copy-start.1 = (f32[2,64,512]{2,1,0:T(8,128)}, f32[2,64,512]{2,1,0:T(8,128)S(1)}, u32[]{:S(2)}) copy-start(f32[2,64,512]{2,1,0:T(8,128)S(1)} %fusion.12) | copy-start | bytes 786436
  130.9 5.5 %collective-permute-start = (f32[2,64,64]{2,1,0:T(8,128)S(1)}, f32[2,64,64]{2,1,0:T(8,128)S(1)}, u32[]{:S(2)}, u32[]{:S(2)}) collective-permute-start(f32[2,64,64]{2,1,0:T(8,128)S(1)} %fusion.18), channel_id=1, source_target_pairs={{0,1},{1,2},{2,3},{3,4},{4,5},{5,6},{6,7},{7,0},{8,9},{9,10},{10,1... | collective-permute-start | bytes 98312 | tf_op jit(solution)/shard_map/ppermute | solution.py:78
  136.4 10.0 %collective-permute-start.1 = (f32[2,64,64]{2,1,0:T(8,128)S(1)}, f32[2,64,64]{2,1,0:T(8,128)S(1)}, u32[]{:S(2)}, u32[]{:S(2)}) collective-permute-start(f32[2,64,64]{2,1,0:T(8,128)S(1)} %collective-permute-done), channel_id=1, source_target_pairs={{0,1},{1,2},{2,3},{3,4},{4,5},{5,6},{6,7},{7,0},{8,9},{9,10},{10,1... | collective-permute-start | bytes 98312 | tf_op jit(solution)/shard_map/ppermute | solution.py:78
  146.4 7.2 %collective-permute-start.2 = (f32[2,64,64]{2,1,0:T(8,128)S(1)}, f32[2,64,64]{2,1,0:T(8,128)S(1)}, u32[]{:S(2)}, u32[]{:S(2)}) collective-permute-start(f32[2,64,64]{2,1,0:T(8,128)S(1)} %collective-permute-done.1), channel_id=1, source_target_pairs={{0,1},{1,2},{2,3},{3,4},{4,5},{5,6},{6,7},{7,0},{8,9},{9,10},{10,1... | collective-permute-start | bytes 98312 | tf_op jit(solution)/shard_map/ppermute | solution.py:78
  153.6 5.5 %collective-permute-start.3 = (f32[2,64,64]{2,1,0:T(8,128)S(1)}, f32[2,64,64]{2,1,0:T(8,128)S(1)}, u32[]{:S(2)}, u32[]{:S(2)}) collective-permute-start(f32[2,64,64]{2,1,0:T(8,128)S(1)} %collective-permute-done.2), channel_id=1, source_target_pairs={{0,1},{1,2},{2,3},{3,4},{4,5},{5,6},{6,7},{7,0},{8,9},{9,10},{10,1... | collective-permute-start | bytes 98312 | tf_op jit(solution)/shard_map/ppermute | solution.py:78
  159.1 5.5 %collective-permute-start.4 = (f32[2,64,64]{2,1,0:T(8,128)S(1)}, f32[2,64,64]{2,1,0:T(8,128)S(1)}, u32[]{:S(2)}, u32[]{:S(2)}) collective-permute-start(f32[2,64,64]{2,1,0:T(8,128)S(1)} %collective-permute-done.3), channel_id=1, source_target_pairs={{0,1},{1,2},{2,3},{3,4},{4,5},{5,6},{6,7},{7,0},{8,9},{9,10},{10,1... | collective-permute-start | bytes 98312 | tf_op jit(solution)/shard_map/ppermute | solution.py:78
  164.6 5.5 %collective-permute-start.5 = (f32[2,64,64]{2,1,0:T(8,128)S(1)}, f32[2,64,64]{2,1,0:T(8,128)S(1)}, u32[]{:S(2)}, u32[]{:S(2)}) collective-permute-start(f32[2,64,64]{2,1,0:T(8,128)S(1)} %collective-permute-done.4), channel_id=1, source_target_pairs={{0,1},{1,2},{2,3},{3,4},{4,5},{5,6},{6,7},{7,0},{8,9},{9,10},{10,1... | collective-permute-start | bytes 98312 | tf_op jit(solution)/shard_map/ppermute | solution.py:78
  170.1 8.7 %collective-permute-start.6 = (f32[2,64,64]{2,1,0:T(8,128)S(1)}, f32[2,64,64]{2,1,0:T(8,128)S(1)}, u32[]{:S(2)}, u32[]{:S(2)}) collective-permute-start(f32[2,64,64]{2,1,0:T(8,128)S(1)} %collective-permute-done.5), channel_id=1, source_target_pairs={{0,1},{1,2},{2,3},{3,4},{4,5},{5,6},{6,7},{7,0},{8,9},{9,10},{10,1... | collective-permute-start | bytes 98312 | tf_op jit(solution)/shard_map/ppermute | solution.py:78
Sparse Core Ops, SparseCore 0:
  49.0 56.7 all-reduce.1
